TPU v7x, 32 devices: a whole 2x2x4 slice. The times are simulated.
32 devices in a mesh: dp: 8 (over z, x), tensor: 4 (over y, core).
Axes of the slice: x: 2, y: 2, z: 4, core: 2. Of those that a mesh axis runs over, the one named last changes fastest.
Arguments:
- tokens: bfloat16 [16384, 1024], P(('dp', 'tensor')), may hold values from -6 to 6
- cotangent: bfloat16 [16384, 1024], P(('dp', 'tensor')), may hold values from -6 to 6
- lengths: int32 [8, 16], P('dp'), may hold values from 1 to 256, 2048 in all within a row
- qkv_master: float32 [1024, 3, 1024], P('dp', None, 'tensor'), may hold values from -0.1875 to 0.1875
- qkv_first: float32 [1024, 3, 1024], P('dp', None, 'tensor'), may hold values from -0.00015258789 to 0.00015258789
- qkv_second: float32 [1024, 3, 1024], P('dp', None, 'tensor'), may hold values from 2.9798684e-11 to 4.7677895e-10
- out_master: float32 [1024, 1024], P(('tensor', 'dp')), may hold values from -1 to 1
- out_first: float32 [1024, 1024], P(('tensor', 'dp')), may hold values from -9.1552734e-05 to 9.1552734e-05
- out_second: float32 [1024, 1024], P(('tensor', 'dp')), may hold values from 5.959737e-12 to 9.535579e-11
- in_master: float32 [1024, 2, 4096], P('dp', None, 'tensor'), may hold values from -0.1875 to 0.1875
- in_first: float32 [1024, 2, 4096], P('dp', None, 'tensor'), may hold values from -0.00015258789 to 0.00015258789
- in_second: float32 [1024, 2, 4096], P('dp', None, 'tensor'), may hold values from 2.9798684e-11 to 4.7677895e-10
- down_master: float32 [4096, 1024], P(('tensor', 'dp')), may hold values from -0.09375 to 0.09375
- down_first: float32 [4096, 1024], P(('tensor', 'dp')), may hold values from -0.00015258789 to 0.00015258789
- down_second: float32 [4096, 1024], P(('tensor', 'dp')), may hold values from 2.9798684e-11 to 4.7677895e-10
- norm_gains: float32 [2, 1024], replicated, may hold values from 0.2 to 2.8
- gain_first: float32 [2, 1024], replicated, may hold values from -0.00061035156 to 0.00061035156
- gain_second: float32 [2, 1024], replicated, may hold values from 4.7677895e-10 to 7.628463e-09
Outputs:
- layer_out: bfloat16 [16384, 1024], P(('dp', 'tensor'))
- input_grad: float32 [16384, 1024], P(('dp', 'tensor'))
- qkv_grad: float32 [1024, 3, 1024], P('dp', None, 'tensor')
- qkv_new: float32 [1024, 3, 1024], P('dp', None, 'tensor')
- qkv_first_new: float32 [1024, 3, 1024], P('dp', None, 'tensor')
- qkv_second_new: float32 [1024, 3, 1024], P('dp', None, 'tensor')
- out_grad: float32 [1024, 1024], P(('tensor', 'dp'))
- out_new: float32 [1024, 1024], P(('tensor', 'dp'))
- out_first_new: float32 [1024, 1024], P(('tensor', 'dp'))
- out_second_new: float32 [1024, 1024], P(('tensor', 'dp'))
- in_grad: float32 [1024, 2, 4096], P('dp', None, 'tensor')
- in_new: float32 [1024, 2, 4096], P('dp', None, 'tensor')
- in_first_new: float32 [1024, 2, 4096], P('dp', None, 'tensor')
- in_second_new: float32 [1024, 2, 4096], P('dp', None, 'tensor')
- down_grad: float32 [4096, 1024], P(('tensor', 'dp'))
- down_new: float32 [4096, 1024], P(('tensor', 'dp'))
- down_first_new: float32 [4096, 1024], P(('tensor', 'dp'))
- down_second_new: float32 [4096, 1024], P(('tensor', 'dp'))
- gain_grad: float32 [2, 1024], replicated
- gain_new: float32 [2, 1024], replicated
- gain_first_new: float32 [2, 1024], replicated
- gain_second_new: float32 [2, 1024], replicated
- grad_norm: float32 [], replicated
Inputs may be any that keep to these rules, and one draw needn't show every extreme that they name: Each row's 16 window lengths are positive, add up to 2048, and the longest is 256.
All inputs are finite; a program needn't handle non-finite values.
Results may differ from a plain program's by a relative error of at most 0.024.
Values may be sent and summed in bfloat16 or wider, within the bound.
No kernel may reach another device: no remote copies, remote signals or barrier semaphores. Data moves between devices by JAX's collectives and lax.ppermute only.
A program may use at most 192 MiB of HBM per device.

v0:
```python
from functools import partial
import math
import jax
import jax.numpy as jnp
from jax import lax
from jax.sharding import PartitionSpec as P

D = 1024
HEADS = 16
HEAD_DIM = 64
FF = 4096
ROW = 2048
STEP = 5
eps_norm = 1e-05
beta_one = 0.9
beta_two = 0.999
learn_rate = 0.05
gain_rate = 0.6
weight_decay = 0.1
adam_eps = 1e-08
max_norm = 1.0


def layer_norm(values, gain):
    centre = values - jnp.mean(values, axis=-1, keepdims=True)
    spread = jnp.mean(centre * centre, axis=-1, keepdims=True)
    return centre * lax.rsqrt(spread + eps_norm) * gain


def row_layout(lengths):
    seg_ends = jnp.cumsum(lengths, axis=-1)
    places = jnp.arange(ROW, dtype=jnp.int32)
    passed = (places[:, None] >= seg_ends[..., None, :]).astype(jnp.int32)
    segment = jnp.sum(passed, axis=-1)
    offset = places - jnp.sum(passed * lengths[..., None, :], axis=-1)
    return (segment, offset)


def rotary_tables(offset):
    half_dim = HEAD_DIM // 2
    inverse = jnp.exp(
        jnp.arange(half_dim, dtype=jnp.float32) * (-2.0 * math.log(10000.0) / HEAD_DIM)
    )
    angles = offset.astype(jnp.float32)[..., None] * inverse
    return (jnp.cos(angles), jnp.sin(angles))


def rotate(values, cosine, sine):
    half_dim = values.shape[-1] // 2
    front_half = values[..., :half_dim]
    back_half = values[..., half_dim:]
    cos_wide = cosine[..., None, :]
    sin_wide = sine[..., None, :]
    return jnp.concatenate(
        [
            front_half * cos_wide - back_half * sin_wide,
            back_half * cos_wide + front_half * sin_wide,
        ],
        axis=-1,
    )


def swiglu(gate_up):
    half_cols = gate_up.shape[-1] // 2
    return jax.nn.silu(gate_up[:, :half_cols]) * gate_up[:, half_cols:]


def adam_update(weight, first_moment, second_moment, gradient, factor, use_decay, rate):
    clipped = gradient * factor
    first_new = beta_one * first_moment + (1.0 - beta_one) * clipped
    second_new = beta_two * second_moment + (1.0 - beta_two) * clipped * clipped
    first_hat = first_new / (1.0 - beta_one**STEP)
    second_hat = second_new / (1.0 - beta_two**STEP)
    direction = first_hat / (jnp.sqrt(second_hat) + adam_eps) + use_decay * weight_decay * weight
    return (clipped, weight - rate * direction, first_new, second_new)


def contract_rows(left, right):
    return lax.dot_general(
        left, right, (((0,), (0,)), ((), ())), preferred_element_type=jnp.float32
    )


def contract_cols(left, right):
    return lax.dot_general(
        left, right, (((1,), (1,)), ((), ())), preferred_element_type=jnp.float32
    )


def per_device(
    tokens,
    cotangent,
    lengths,
    qkv_master,
    qkv_first,
    qkv_second,
    out_master,
    out_first,
    out_second,
    in_master,
    in_first,
    in_second,
    down_master,
    down_first,
    down_second,
    norm_gains,
    gain_first,
    gain_second,
):
    heads_local = HEADS // lax.axis_size("tensor")
    width_local = heads_local * HEAD_DIM
    ffn_local = FF // lax.axis_size("tensor")
    row_count = lengths.shape[0]
    all_rows = row_count * ROW
    score_scale = HEAD_DIM ** (-0.5)
    block_rows = min(512, ROW)
    block_count = ROW // block_rows
    w_qkv, w_out, w_in, w_down = (
        lax.all_gather(qkv_master.astype(jnp.bfloat16), "dp", axis=0, tiled=True),
        lax.all_gather(out_master.astype(jnp.bfloat16), "dp", axis=0, tiled=True),
        lax.all_gather(in_master.astype(jnp.bfloat16), "dp", axis=0, tiled=True),
        lax.all_gather(down_master.astype(jnp.bfloat16), "dp", axis=0, tiled=True),
    )
    w_qkv = w_qkv.reshape(D, 3 * width_local)
    w_in = w_in.reshape(D, 2 * ffn_local)
    segment, offset = row_layout(lengths)
    cosine, sine = rotary_tables(offset)
    gain_one = norm_gains[0]
    gain_two = norm_gains[1]
    inputs = tokens.astype(jnp.float32)
    normed = layer_norm(inputs, gain_one)
    gathered_one = lax.all_gather(normed.astype(jnp.bfloat16), "tensor", axis=0, tiled=True)
    projected = jnp.dot(gathered_one, w_qkv, preferred_element_type=jnp.float32)
    projected = projected.reshape(row_count, ROW, 3, heads_local, HEAD_DIM)
    queries = rotate(projected[:, :, 0], cosine, sine).astype(jnp.bfloat16)
    keys = rotate(projected[:, :, 1], cosine, sine).astype(jnp.bfloat16)
    values = projected[:, :, 2].astype(jnp.bfloat16)

    def score_block(query_block, key_row, segment_block, segment_row):
        scores = (
            jnp.einsum("qhd,khd->hqk", query_block, key_row, preferred_element_type=jnp.float32)
            * score_scale
        )
        allowed = segment_block[:, None] == segment_row[None, :]
        return jnp.where(allowed[None], scores, -1e30)

    def forward_row(pieces):
        query_row, key_row, value_row, segment_row = pieces

        def forward_block(block_parts):
            query_block, segment_block = block_parts
            masked = score_block(query_block, key_row, segment_block, segment_row)
            row_max = jnp.max(masked, axis=-1, keepdims=True)
            log_total = (
                jnp.log(jnp.sum(jnp.exp(masked - row_max), axis=-1, keepdims=True)) + row_max
            )
            weights = jnp.exp(masked - log_total).astype(jnp.bfloat16)
            mixed_heads = jnp.einsum(
                "hqk,khd->qhd", weights, value_row, preferred_element_type=jnp.float32
            )
            return (mixed_heads.astype(jnp.bfloat16), log_total)

        return lax.map(
            forward_block,
            (
                query_row.reshape(block_count, block_rows, heads_local, HEAD_DIM),
                segment_row.reshape(block_count, block_rows),
            ),
        )

    mixed_heads, log_totals = lax.map(forward_row, (queries, keys, values, segment))
    attended = mixed_heads.reshape(all_rows, width_local)
    middle = inputs + lax.psum_scatter(
        jnp.dot(attended, w_out, preferred_element_type=jnp.float32),
        "tensor",
        scatter_dimension=0,
        tiled=True,
    )
    normed_two = layer_norm(middle, gain_two)
    gathered_two = lax.all_gather(normed_two.astype(jnp.bfloat16), "tensor", axis=0, tiled=True)
    gate_up = jnp.dot(gathered_two, w_in, preferred_element_type=jnp.float32)
    hidden = swiglu(gate_up).astype(jnp.bfloat16)
    output = middle + lax.psum_scatter(
        jnp.dot(hidden, w_down, preferred_element_type=jnp.float32).astype(jnp.bfloat16),
        "tensor",
        scatter_dimension=0,
        tiled=True,
    ).astype(jnp.float32)
    layer_out = output.astype(jnp.bfloat16)
    upstream = cotangent.astype(jnp.float32)
    gathered_down = lax.all_gather(cotangent, "tensor", axis=0, tiled=True)
    grad_down = contract_rows(hidden, gathered_down)
    hidden_grad = contract_cols(gathered_down, w_down)
    gate_up_grad = jax.vjp(swiglu, gate_up)[1](hidden_grad)[0].astype(jnp.bfloat16)
    grad_in = contract_rows(gathered_two, gate_up_grad)
    normed_two_grad = lax.psum_scatter(
        contract_cols(gate_up_grad, w_in).astype(jnp.bfloat16),
        "tensor",
        scatter_dimension=0,
        tiled=True,
    ).astype(jnp.float32)
    middle_back, gain_two_grad = jax.vjp(layer_norm, middle, gain_two)[1](normed_two_grad)
    middle_grad = upstream + middle_back
    gathered_mid = lax.all_gather(middle_grad.astype(jnp.bfloat16), "tensor", axis=0, tiled=True)
    grad_out = contract_rows(attended, gathered_mid)
    attended_grad = contract_cols(gathered_mid, w_out).astype(jnp.bfloat16)
    attended_grad = attended_grad.reshape(row_count, ROW, heads_local, HEAD_DIM)

    def backward_row(pieces):
        query_row, key_row, value_row, segment_row, total_row, grad_row = pieces

        def backward_block(running, block_parts):
            key_acc, value_acc = running
            query_block, segment_block, total_block, grad_block = block_parts
            masked = score_block(query_block, key_row, segment_block, segment_row)
            probs_block = jnp.exp(masked - total_block)
            probs_low = probs_block.astype(jnp.bfloat16)
            prob_grad = jnp.einsum(
                "qhd,khd->hqk", grad_block, value_row, preferred_element_type=jnp.float32
            )
            row_inner = jnp.sum(probs_block * prob_grad, axis=-1, keepdims=True)
            score_grad = (probs_block * (prob_grad - row_inner)).astype(jnp.bfloat16)
            query_grad = (
                jnp.einsum("hqk,khd->qhd", score_grad, key_row, preferred_element_type=jnp.float32)
                * score_scale
            )
            key_acc = (
                key_acc
                + jnp.einsum(
                    "hqk,qhd->khd", score_grad, query_block, preferred_element_type=jnp.float32
                )
                * score_scale
            )
            value_acc = value_acc + jnp.einsum(
                "hqk,qhd->khd", probs_low, grad_block, preferred_element_type=jnp.float32
            )
            return ((key_acc, value_acc), query_grad)

        zeros_acc = jnp.zeros((ROW, heads_local, HEAD_DIM), jnp.float32)
        block_inputs = (
            query_row.reshape(block_count, block_rows, heads_local, HEAD_DIM),
            segment_row.reshape(block_count, block_rows),
            total_row,
            grad_row.reshape(block_count, block_rows, heads_local, HEAD_DIM),
        )
        (key_grad, value_grad), query_grad = lax.scan(
            backward_block, (zeros_acc, zeros_acc), block_inputs
        )
        return (query_grad.reshape(ROW, heads_local, HEAD_DIM), key_grad, value_grad)

    query_grad, key_grad, value_grad = lax.map(
        backward_row, (queries, keys, values, segment, log_totals, attended_grad)
    )
    rotate_back = jax.vjp(partial(rotate, cosine=cosine, sine=sine), projected[:, :, 0])[1]
    query_raw = rotate_back(query_grad)[0]
    key_raw = rotate_back(key_grad)[0]
    qkv_grad_low = (
        jnp.stack([query_raw, key_raw, value_grad], axis=2)
        .reshape(all_rows, 3 * width_local)
        .astype(jnp.bfloat16)
    )
    grad_qkv = contract_rows(gathered_one, qkv_grad_low)
    normed_grad = lax.psum_scatter(
        contract_cols(qkv_grad_low, w_qkv).astype(jnp.bfloat16),
        "tensor",
        scatter_dimension=0,
        tiled=True,
    ).astype(jnp.float32)
    input_back, gain_one_grad = jax.vjp(layer_norm, inputs, gain_one)[1](normed_grad)
    input_grad = middle_grad + input_back
    reduced_qkv, reduced_out, reduced_in, reduced_down = (
        lax.psum_scatter(
            grad_qkv.reshape(D, 3, width_local).astype(jnp.bfloat16),
            "dp",
            scatter_dimension=0,
            tiled=True,
        ).astype(jnp.float32),
        lax.psum_scatter(
            grad_out.astype(jnp.bfloat16), "dp", scatter_dimension=0, tiled=True
        ).astype(jnp.float32),
        lax.psum_scatter(
            grad_in.reshape(D, 2, ffn_local).astype(jnp.bfloat16),
            "dp",
            scatter_dimension=0,
            tiled=True,
        ).astype(jnp.float32),
        lax.psum_scatter(
            grad_down.astype(jnp.bfloat16), "dp", scatter_dimension=0, tiled=True
        ).astype(jnp.float32),
    )
    local_squares = (
        jnp.sum(reduced_qkv * reduced_qkv)
        + jnp.sum(reduced_out * reduced_out)
        + jnp.sum(reduced_in * reduced_in)
        + jnp.sum(reduced_down * reduced_down)
    )
    gain_part = jnp.stack([gain_one_grad, gain_two_grad])
    gain_total, weight_squares = lax.psum((gain_part, local_squares), ("dp", "tensor"))
    grad_norm = jnp.sqrt(weight_squares + jnp.sum(gain_total * gain_total))
    factor = max_norm / jnp.maximum(grad_norm, max_norm)
    qkv_res = adam_update(qkv_master, qkv_first, qkv_second, reduced_qkv, factor, 1.0, learn_rate)
    out_res = adam_update(out_master, out_first, out_second, reduced_out, factor, 1.0, learn_rate)
    in_res = adam_update(in_master, in_first, in_second, reduced_in, factor, 1.0, learn_rate)
    down_res = adam_update(
        down_master, down_first, down_second, reduced_down, factor, 1.0, learn_rate
    )
    gain_res = adam_update(norm_gains, gain_first, gain_second, gain_total, factor, 0.0, gain_rate)
    return (
        layer_out,
        input_grad,
        qkv_res[0],
        qkv_res[1],
        qkv_res[2],
        qkv_res[3],
        out_res[0],
        out_res[1],
        out_res[2],
        out_res[3],
        in_res[0],
        in_res[1],
        in_res[2],
        in_res[3],
        down_res[0],
        down_res[1],
        down_res[2],
        down_res[3],
        gain_res[0],
        gain_res[1],
        gain_res[2],
        gain_res[3],
        grad_norm,
    )


def solution(mesh):
    placed = (
        P(("dp", "tensor"), None),
        P(("dp", "tensor"), None),
        P("dp", None),
        P("dp", None, "tensor"),
        P("dp", None, "tensor"),
        P("dp", None, "tensor"),
        P(("tensor", "dp"), None),
        P(("tensor", "dp"), None),
        P(("tensor", "dp"), None),
        P("dp", None, "tensor"),
        P("dp", None, "tensor"),
        P("dp", None, "tensor"),
        P(("tensor", "dp"), None),
        P(("tensor", "dp"), None),
        P(("tensor", "dp"), None),
        P(),
        P(),
        P(),
    )
    return jax.shard_map(
        per_device,
        mesh=mesh,
        in_specs=placed,
        out_specs=(
            P(("dp", "tensor"), None),
            P(("dp", "tensor"), None),
            P("dp", None, "tensor"),
            P("dp", None, "tensor"),
            P("dp", None, "tensor"),
            P("dp", None, "tensor"),
            P(("tensor", "dp"), None),
            P(("tensor", "dp"), None),
            P(("tensor", "dp"), None),
            P(("tensor", "dp"), None),
            P("dp", None, "tensor"),
            P("dp", None, "tensor"),
            P("dp", None, "tensor"),
            P("dp", None, "tensor"),
            P(("tensor", "dp"), None),
            P(("tensor", "dp"), None),
            P(("tensor", "dp"), None),
            P(("tensor", "dp"), None),
            P(),
            P(),
            P(),
            P(),
            P(),
        ),
        check_vma=False,
    )
```

profile of v0, /device:TPU:0, one launch (start us, length us, event | category | flops | bytes accessed | tf_op | source)
XLA Modules:
  0.0 1104.4 jit_solution(1875028781626215786)
XLA Ops:
  16.8 36.3 %all_gather.26 = bf16[256,1024]{1,0:T(8,128)(2,1)} all-gather(bf16[32,1024]{1,0:T(8,128)(2,1)S(1)} %convert_element_type.159), channel_id=1, replica_groups=mesh['dp'=8,'tensor'=4] {'dp'}, dimensions={0}, use_global_device_ids=true | all-gather | bytes 589824 | tf_op jit(solution)/shard_map/all_gather | solution.py:120
  54.1 7.5 all-gather.10.cloned.1.call-done
  61.6 35.9 %all-gather.8.cloned.1.call-done = bf16[2048,1024]{1,0:T(8,128)(2,1)} async-done(((bf16[512,1024]{1,0:T(8,128)(2,1)}), bf16[2048,1024]{1,0:T(8,128)(2,1)}) %all-gather.8.cloned.1.call-update) | async-done | bytes 4194320 | tf_op jit(solution)/shard_map/all_gather | solution.py:132
  97.5 6.2 fusion.48
  110.1 57.2 %while.47 = (s32[]{:T(128)}, bf16[4,512,4,64]{1,3,2,0:T(8,128)(2,1)}, f32[4,4,512,1]{2,1,3,0:T(4,128)}, s32[4,512]{1,0:T(4,128)S(1)}, s32[2048]{0:T(1024)S(1)}, ...) while((s32[]{:T(128)}, ...), condition=%wide.region_8.9_spmd, body=%wide.region_5.8_spmd.sunk | while | flops 1121056768 | bytes 57227380 | solution.py:163
  119.0 5.5 fusion.144
  178.4 69.5 %reduce-scatter.8.cloned.1.call-done = f32[512,1024]{1,0:T(8,128)} async-done(((f32[2048,1024]{1,0:T(8,128)}), f32[512,1024]{1,0:T(8,128)}) %reduce-scatter.8.cloned.1.call-update) | async-done | bytes 2097168 | tf_op jit(solution)/shard_map/reduce_scatter | solution.py:173
  254.4 69.7 %all-gather.14.cloned.1.call-done = bf16[1024,2,1024]{2,1,0:T(2,128)(2,1)} async-done(((bf16[128,2,1024]{2,1,0:T(2,128)(2,1)}), bf16[1024,2,1024]{2,1,0:T(2,128)(2,1)}) %all-gather.14.cloned.1.call-update) | async-done | bytes 4194320 | tf_op jit(solution)/shard_map/all_gather | solution.py:121
  324.1 5.6 copy.103
  329.7 29.2 %all-gather.12.cloned.1.call-done = bf16[2048,1024]{1,0:T(8,128)(2,1)} async-done(((bf16[512,1024]{1,0:T(8,128)(2,1)}), bf16[2048,1024]{1,0:T(8,128)(2,1)}) %all-gather.12.cloned.1.call-update) | async-done | bytes 4194320 | tf_op jit(solution)/shard_map/all_gather | solution.py:180
  358.9 15.1 %fusion.96 = f32[2048,2048]{1,0:T(8,128)} fusion(bf16[2048,1024]{1,0:T(8,128)(2,1)} %all-gather.12.cloned.1.call-done, bf16[1024,2048]{1,0:T(8,128)(2,1)} %bitcast.176), kind=kOutput, calls=%fused_computation.180 | convolution fusion | flops 8589934592 | bytes 25165824 | tf_op jit(solution)/shard_map/dot_general | solution.py:181
  374.0 37.0 %all-gather.16.cloned.1.call-done = bf16[1024,1024]{1,0:T(8,128)(2,1)} async-done(((bf16[128,1024]{1,0:T(8,128)(2,1)}), bf16[1024,1024]{1,0:T(8,128)(2,1)}) %all-gather.16.cloned.1.call-update) | async-done | bytes 2097168 | tf_op jit(solution)/shard_map/all_gather | solution.py:122
  411.0 34.6 %all-gather.18.cloned.1.call-done = bf16[2048,1024]{1,0:T(8,128)(2,1)} async-done(((bf16[512,1024]{1,0:T(8,128)(2,1)}), bf16[2048,1024]{1,0:T(8,128)(2,1)}) %all-gather.18.cloned.1.call-update) | async-done | bytes 4194320 | tf_op jit(solution)/shard_map/all_gather | solution.py:191
  445.6 17.2 %fusion.73 = (f32[2048,1024]{1,0:T(8,128)}, f32[2048,1024]{1,0:T(8,128)}, bf16[2048,1024]{1,0:T(8,128)(2,1)}) fusion(f32[2048,2048]{1,0:T(8,128)} %fusion.96, bf16[2048,1024]{1,0:T(8,128)(2,1)} %all-gather.18.cloned.1.call-done, bf16[1024,1024]{1,0:T(8,128)(2,1)} %all-gather.16.cloned.1.call-done), kind=kOutput, calls=%fused_computation.124 | convolution fusion | flops 4324327424 | bytes 44040192 | tf_op jit(solution)/shard_map/dot_general | solution.py:85
  462.8 15.0 %convolution_convert_fusion.1 = bf16[2048,1024]{1,0:T(8,128)(2,1)} fusion(bf16[1024,2048]{1,0:T(8,128)(2,1)} %bitcast.177, f32[2048,1024]{1,0:T(8,128)} %get-tuple-element.338, f32[2048,1024]{1,0:T(8,128)} %get-tuple-element.337), kind=kOutput, calls=%fused_computation.65 | convolution fusion | flops 8600420352 | bytes 25165824 | tf_op jit(solution)/shard_map/dot_general | solution.py:85
  478.4 9.6 convolution_convert_fusion.3
  488.0 34.6 %reduce-scatter.12.cloned.1.call-done = bf16[512,1024]{1,0:T(8,128)(2,1)} async-done(((bf16[2048,1024]{1,0:T(8,128)(2,1)}), bf16[512,1024]{1,0:T(8,128)(2,1)}) %reduce-scatter.12.cloned.1.call-update) | async-done | bytes 1048592 | tf_op jit(solution)/shard_map/reduce_scatter | solution.py:196
  525.3 44.4 %reduce-scatter.10.cloned.1.call-done = bf16[512,1024]{1,0:T(8,128)(2,1)} async-done(((bf16[2048,1024]{1,0:T(8,128)(2,1)}), bf16[512,1024]{1,0:T(8,128)(2,1)}) %reduce-scatter.10.cloned.1.call-update) | async-done | bytes 1048592 | tf_op jit(solution)/shard_map/reduce_scatter | solution.py:183
  575.8 17.0 %convolution_convert_fusion = bf16[1024,2048]{1,0:T(8,128)(2,1)} fusion(bf16[2048,1024]{1,0:T(8,128)(2,1)} %all-gather.12.cloned.1.call-done, f32[2048,1024]{1,0:T(8,128)} %get-tuple-element.338, f32[2048,1024]{1,0:T(8,128)} %get-tuple-element.337), kind=kOutput, calls=%fused_computation.64 | convolution fusion | flops 8600420352 | bytes 25165824 | tf_op jit(solution)/shard_map/dot_general | solution.py:79
  592.8 7.9 convert_element_type.182
  600.8 9.4 convolution_convert_fusion.5
  620.5 230.1 %while.48 = (s32[]{:T(128)}, f32[2048,4,64]{0,2,1:T(8,128)}, f32[2048,4,64]{0,2,1:T(8,128)}, f32[4,512,4,64]{1,0,3,2:T(4,128)}, bf16[4,512,4,64]{1,3,2,0:T(8,128...) while((s32[]{:T(128)}, f32[2048,4,64]{0,2,1:T(8,128)}, ...), condition=%wide.region_18.19_spmd.clone, body=%wide.region_16.18_spmd.clone.sunk | while | flops 2751068160 | bytes 183179600 | solution.py:246
  625.6 7.2 fusion.156
  632.8 11.5 %multiply_reduce_fusion.4 = (f32[4,512]{1,0:T(4,128)}, f32[4,512,2048]{2,1,0:T(8,128)}) fusion(f32[4,512,2048]{2,1,0:T(8,128)S(1)} %fusion.154, f32[4,512]{1,0:T(4,128)S(1)} %dynamic-slice_bitcast_fusion.2, pred[512,2048]{1,0:T(8,128)(4,1)} %copy-done.1, bf16[2048,4,64]{0,2,1:T(8,128)(2,1)} %get-tuple-element.552, ...), kind=kOutput, calls=%fused_computation.20.clone.1 | convolution fusion | flops 557840384 | bytes 35930116 | tf_op jit(solution)/shard_map/while/body/eval_jaxpr/while/body/eval_jaxpr/qhd,khd->hqk/dot_general | solution.py:218
  644.4 11.2 %multiply_convert_fusion.4 = bf16[4,512,2048]{2,1,0:T(8,128)(2,1)} fusion(f32[4,512,2048]{2,1,0:T(8,128)} %get-tuple-element.487, f32[4,512,2048]{2,1,0:T(8,128)S(1)} %fusion.154, f32[4,512]{1,0:T(4,128)} %get-tuple-element.488, f32[4,512]{1,0:T(4,128)S(1)} %dynamic-slice_bitcast_fusion.2, pred[512,2048]{1,0:T(8,128)(4,1)} %copy-done.1), kind=kLoop, calls=%fused_computation.19.clone.1 | loop fusion | flops 25165824 | bytes 43008000 | tf_op jit(solution)/shard_map/while/body/eval_jaxpr/while/body/eval_jaxpr/convert_element_type | solution.py:222
  655.5 6.2 fusion.157
  666.2 11.1 %dynamic_update_slice.33 = f32[4,512,4,64]{1,0,3,2:T(4,128)} dynamic-update-slice(f32[4,512,4,64]{1,0,3,2:T(4,128)} %get-tuple-element.532, f32[1,512,4,64]{1,0,3,2:T(1,128)S(1)} %copy.107, s32[]{:T(128)S(6)} %copy.125, s32[]{:T(128)} %constant.79.clone.1..sunk, s32[]{:T(128)} %constant.79.clone.1..sunk, s32[]{:T(128)} %constant.79.clone.1..sunk) | dynamic-update-slice | bytes 1048580 | tf_op jit(solution)/shard_map/while/body/eval_jaxpr/while/body/jit(dynamic_update_index_in_dim)/dynamic_update_slice | solution.py:246
  682.2 7.6 fusion.156
  689.9 11.5 %multiply_reduce_fusion.4 = (f32[4,512]{1,0:T(4,128)}, f32[4,512,2048]{2,1,0:T(8,128)}) fusion(f32[4,512,2048]{2,1,0:T(8,128)S(1)} %fusion.154, f32[4,512]{1,0:T(4,128)S(1)} %dynamic-slice_bitcast_fusion.2, pred[512,2048]{1,0:T(8,128)(4,1)} %copy-done.1, bf16[2048,4,64]{0,2,1:T(8,128)(2,1)} %get-tuple-element.552, ...), kind=kOutput, calls=%fused_computation.20.clone.1 | convolution fusion | flops 557840384 | bytes 35930116 | tf_op jit(solution)/shard_map/while/body/eval_jaxpr/while/body/eval_jaxpr/qhd,khd->hqk/dot_general | solution.py:218
  701.4 11.0 %multiply_convert_fusion.4 = bf16[4,512,2048]{2,1,0:T(8,128)(2,1)} fusion(f32[4,512,2048]{2,1,0:T(8,128)} %get-tuple-element.487, f32[4,512,2048]{2,1,0:T(8,128)S(1)} %fusion.154, f32[4,512]{1,0:T(4,128)} %get-tuple-element.488, f32[4,512]{1,0:T(4,128)S(1)} %dynamic-slice_bitcast_fusion.2, pred[512,2048]{1,0:T(8,128)(4,1)} %copy-done.1), kind=kLoop, calls=%fused_computation.19.clone.1 | loop fusion | flops 25165824 | bytes 43008000 | tf_op jit(solution)/shard_map/while/body/eval_jaxpr/while/body/eval_jaxpr/convert_element_type | solution.py:222
  712.5 6.2 fusion.157
  723.9 11.1 %dynamic_update_slice.33 = f32[4,512,4,64]{1,0,3,2:T(4,128)} dynamic-update-slice(f32[4,512,4,64]{1,0,3,2:T(4,128)} %get-tuple-element.532, f32[1,512,4,64]{1,0,3,2:T(1,128)S(1)} %copy.107, s32[]{:T(128)S(6)} %copy.125, s32[]{:T(128)} %constant.79.clone.1..sunk, s32[]{:T(128)} %constant.79.clone.1..sunk, s32[]{:T(128)} %constant.79.clone.1..sunk) | dynamic-update-slice | bytes 1048580 | tf_op jit(solution)/shard_map/while/body/eval_jaxpr/while/body/jit(dynamic_update_index_in_dim)/dynamic_update_slice | solution.py:246
  740.0 7.6 fusion.156
  747.6 11.5 %multiply_reduce_fusion.4 = (f32[4,512]{1,0:T(4,128)}, f32[4,512,2048]{2,1,0:T(8,128)}) fusion(f32[4,512,2048]{2,1,0:T(8,128)S(1)} %fusion.154, f32[4,512]{1,0:T(4,128)S(1)} %dynamic-slice_bitcast_fusion.2, pred[512,2048]{1,0:T(8,128)(4,1)} %copy-done.1, bf16[2048,4,64]{0,2,1:T(8,128)(2,1)} %get-tuple-element.552, ...), kind=kOutput, calls=%fused_computation.20.clone.1 | convolution fusion | flops 557840384 | bytes 35930116 | tf_op jit(solution)/shard_map/while/body/eval_jaxpr/while/body/eval_jaxpr/qhd,khd->hqk/dot_general | solution.py:218
  759.2 11.0 multiply_convert_fusion.4
  770.2 6.2 fusion.157
  781.6 11.1 %dynamic_update_slice.33 = f32[4,512,4,64]{1,0,3,2:T(4,128)} dynamic-update-slice(f32[4,512,4,64]{1,0,3,2:T(4,128)} %get-tuple-element.532, f32[1,512,4,64]{1,0,3,2:T(1,128)S(1)} %copy.107, s32[]{:T(128)S(6)} %copy.125, s32[]{:T(128)} %constant.79.clone.1..sunk, s32[]{:T(128)} %constant.79.clone.1..sunk, s32[]{:T(128)} %constant.79.clone.1..sunk) | dynamic-update-slice | bytes 1048580 | tf_op jit(solution)/shard_map/while/body/eval_jaxpr/while/body/jit(dynamic_update_index_in_dim)/dynamic_update_slice | solution.py:246
  797.6 7.6 fusion.156
  805.3 11.5 %multiply_reduce_fusion.4 = (f32[4,512]{1,0:T(4,128)}, f32[4,512,2048]{2,1,0:T(8,128)}) fusion(f32[4,512,2048]{2,1,0:T(8,128)S(1)} %fusion.154, f32[4,512]{1,0:T(4,128)S(1)} %dynamic-slice_bitcast_fusion.2, pred[512,2048]{1,0:T(8,128)(4,1)} %copy-done.1, bf16[2048,4,64]{0,2,1:T(8,128)(2,1)} %get-tuple-element.552, ...), kind=kOutput, calls=%fused_computation.20.clone.1 | convolution fusion | flops 557840384 | bytes 35930116 | tf_op jit(solution)/shard_map/while/body/eval_jaxpr/while/body/eval_jaxpr/qhd,khd->hqk/dot_general | solution.py:218
  816.8 11.0 multiply_convert_fusion.4
  827.9 6.2 fusion.157
  839.3 11.1 %dynamic_update_slice.33 = f32[4,512,4,64]{1,0,3,2:T(4,128)} dynamic-update-slice(f32[4,512,4,64]{1,0,3,2:T(4,128)} %get-tuple-element.532, f32[1,512,4,64]{1,0,3,2:T(1,128)S(1)} %copy.107, s32[]{:T(128)S(6)} %copy.125, s32[]{:T(128)} %constant.79.clone.1..sunk, s32[]{:T(128)} %constant.79.clone.1..sunk, s32[]{:T(128)} %constant.79.clone.1..sunk) | dynamic-update-slice | bytes 1048580 | tf_op jit(solution)/shard_map/while/body/eval_jaxpr/while/body/jit(dynamic_update_index_in_dim)/dynamic_update_slice | solution.py:246
  870.1 7.0 convolution_convert_fusion.2
  883.5 37.6 %reduce-scatter.18.cloned.1.call-done = bf16[32,1024]{1,0:T(8,128)(2,1)} async-done(((bf16[256,1024]{1,0:T(8,128)(2,1)}), bf16[32,1024]{1,0:T(8,128)(2,1)}) %reduce-scatter.18.cloned.1.call-update) | async-done | bytes 65552 | tf_op jit(solution)/shard_map/reduce_scatter | solution.py:278
  922.6 66.9 %reduce-scatter.16.cloned.1.call-done = bf16[128,3,256]{2,0,1:T(8,128)(2,1)} async-done(((bf16[1024,3,256]{2,0,1:T(8,128)(2,1)}), bf16[128,3,256]{2,0,1:T(8,128)(2,1)}) %reduce-scatter.16.cloned.1.call-update) | async-done | bytes 196624 | tf_op jit(solution)/shard_map/reduce_scatter | solution.py:272
  993.7 41.8 %reduce-scatter.14.cloned.1.call-done = bf16[512,1024]{1,0:T(8,128)(2,1)} async-done(((bf16[2048,1024]{1,0:T(8,128)(2,1)}), bf16[512,1024]{1,0:T(8,128)(2,1)}) %reduce-scatter.14.cloned.1.call-update) | async-done | bytes 1048592 | tf_op jit(solution)/shard_map/reduce_scatter | solution.py:263
  1039.7 39.7 %all-reduce.7 = (f32[]{:T(128)}, f32[2,1024]{1,0:T(2,128)S(1)}) all-reduce(f32[]{:T(128)S(6)} %add.210, f32[2,1024]{1,0:T(2,128)S(1)} %pad_maximum_fusion.1), channel_id=1, replica_groups=mesh['dp'=8,'tensor'=4] {'dp','tensor'}, use_global_device_ids=true, to_apply=%region_30.31 | all-reduce | flops 2049 | bytes 16392 | tf_op jit(solution)/shard_map/psum | solution.py:298
  1086.4 6.5 multiply_subtract_fusion
  (297 shorter events, 186.4 us)
Async XLA Ops:
  7.2 9.1 copy-start.52
  7.2 9.6 copy-start.29
  7.2 54.4 %all-gather.10.cloned.1.call-start = ((), (), s32[]{:S(2)}) async-start(), calls=%async_computation.8 | async-start | bytes 1769472 | tf_op jit(solution)/shard_map/all_gather | solution.py:119
  9.1 88.4 %all-gather.8.cloned.1.call-start = ((), (), s32[]{:S(2)}) async-start(), calls=%async_computation.7 | async-start | bytes 5242880 | tf_op jit(solution)/shard_map/all_gather | solution.py:132
  16.3 231.6 %reduce-scatter.8.cloned.1.call-start = ((), (), s32[]{:S(2)}) async-start(), calls=%async_computation.9 | async-start | bytes 10485760 | tf_op jit(solution)/shard_map/reduce_scatter | solution.py:173
  54.1 50.3 %copy-start.14 = (f32[2048,32]{0,1:T(8,128)}, f32[2048,32]{0,1:T(8,128)S(1)}, u32[]{:S(2)}) copy-start(f32[2048,32]{0,1:T(8,128)S(1)} %get-tuple-element.355) | copy-start | bytes 786436
  54.1 50.3 %copy-start.16 = (f32[2048,32]{0,1:T(8,128)}, f32[2048,32]{0,1:T(8,128)S(1)}, u32[]{:S(2)}) copy-start(f32[2048,32]{0,1:T(8,128)S(1)} %get-tuple-element.356) | copy-start | bytes 786436
  167.3 8.6 copy-start.4
  167.3 8.6 copy-start.5
  176.0 148.1 %all-gather.14.cloned.1.call-start = ((), (), s32[]{:S(2)}) async-start(), calls=%async_computation.11 | async-start | bytes 4718592 | tf_op jit(solution)/shard_map/all_gather | solution.py:121
  178.4 180.5 %all-gather.12.cloned.1.call-start = ((), (), s32[]{:S(2)}) async-start(), calls=%async_computation.10 | async-start | bytes 5242880 | tf_op jit(solution)/shard_map/all_gather | solution.py:180
  251.7 159.3 %all-gather.16.cloned.1.call-start = ((), (), s32[]{:S(2)}) async-start(), calls=%async_computation.12 | async-start | bytes 2359296 | tf_op jit(solution)/shard_map/all_gather | solution.py:122
  253.6 192.1 %all-gather.18.cloned.1.call-start = ((), (), s32[]{:S(2)}) async-start(), calls=%async_computation.14 | async-start | bytes 5242880 | tf_op jit(solution)/shard_map/all_gather | solution.py:191
  254.3 268.3 %reduce-scatter.12.cloned.1.call-start = ((), (), s32[]{:S(2)}) async-start(), calls=%async_computation.15 | async-start | bytes 5242880 | tf_op jit(solution)/shard_map/reduce_scatter | solution.py:196
  477.9 91.8 %reduce-scatter.10.cloned.1.call-start = ((), (), s32[]{:S(2)}) async-start(), calls=%async_computation.13 | async-start | bytes 5242880 | tf_op jit(solution)/shard_map/reduce_scatter | solution.py:183
  488.0 122.4 %all-gather.20.cloned.1.call-start = ((), (), s32[]{:S(2)}) async-start(), calls=%async_computation.16 | async-start | bytes 5242880 | tf_op jit(solution)/shard_map/all_gather | solution.py:204
  573.1 19.7 %copy-start.45 = (f32[512]{0:T(512)}, f32[512]{0:T(512)S(1)}, u32[]{:S(2)}) copy-start(f32[512]{0:T(512)S(1)} %negate_multiply_fusion.1) | copy-start | bytes 6148
  575.7 303.3 %all-reduce.10.cloned.1.call-start = ((), (), s32[]{:S(2)}) async-start(), calls=%async_computation.21 | async-start | bytes 8388608
  600.7 281.1 %reduce-scatter.20.cloned.1.call-start = ((), (), s32[]{:S(2)}) async-start(), calls=%async_computation.20 | async-start | bytes 2359296 | tf_op jit(solution)/shard_map/reduce_scatter | solution.py:287
  600.8 9.6 copy-start.19
  610.3 310.8 %reduce-scatter.18.cloned.1.call-start = ((), (), s32[]{:S(2)}) async-start(), calls=%async_computation.19 | async-start | bytes 589824 | tf_op jit(solution)/shard_map/reduce_scatter | solution.py:278
  661.7 15.6 %copy-start.22 = (s32[2048]{0:T(1024)S(1)}, s32[2048]{0:T(1024)}, u32[]{:S(2)}) copy-start(s32[2048]{0:T(1024)} %copy-done.21) | copy-start | bytes 24580 | tf_op jit(solution)/shard_map/while/body/eval_jaxpr/while
  661.7 15.6 %copy-start.39 = (s32[4,512]{1,0:T(4,128)S(1)}, s32[4,512]{1,0:T(4,128)}, u32[]{:S(2)}) copy-start(s32[4,512]{1,0:T(4,128)} %copy-done.38) | copy-start | bytes 24580 | tf_op jit(solution)/shard_map/while/body/eval_jaxpr/while
  718.7 16.4 %copy-start.22 = (s32[2048]{0:T(1024)S(1)}, s32[2048]{0:T(1024)}, u32[]{:S(2)}) copy-start(s32[2048]{0:T(1024)} %copy-done.21) | copy-start | bytes 24580 | tf_op jit(solution)/shard_map/while/body/eval_jaxpr/while
  718.7 16.4 %copy-start.39 = (s32[4,512]{1,0:T(4,128)S(1)}, s32[4,512]{1,0:T(4,128)}, u32[]{:S(2)}) copy-start(s32[4,512]{1,0:T(4,128)} %copy-done.38) | copy-start | bytes 24580 | tf_op jit(solution)/shard_map/while/body/eval_jaxpr/while
  776.4 16.3 %copy-start.22 = (s32[2048]{0:T(1024)S(1)}, s32[2048]{0:T(1024)}, u32[]{:S(2)}) copy-start(s32[2048]{0:T(1024)} %copy-done.21) | copy-start | bytes 24580 | tf_op jit(solution)/shard_map/while/body/eval_jaxpr/while
  776.4 16.3 %copy-start.39 = (s32[4,512]{1,0:T(4,128)S(1)}, s32[4,512]{1,0:T(4,128)}, u32[]{:S(2)}) copy-start(s32[4,512]{1,0:T(4,128)} %copy-done.38) | copy-start | bytes 24580 | tf_op jit(solution)/shard_map/while/body/eval_jaxpr/while
  834.1 16.3 %copy-start.22 = (s32[2048]{0:T(1024)S(1)}, s32[2048]{0:T(1024)}, u32[]{:S(2)}) copy-start(s32[2048]{0:T(1024)} %copy-done.21) | copy-start | bytes 24580 | tf_op jit(solution)/shard_map/while/body/eval_jaxpr/while
  834.1 16.3 %copy-start.39 = (s32[4,512]{1,0:T(4,128)S(1)}, s32[4,512]{1,0:T(4,128)}, u32[]{:S(2)}) copy-start(s32[4,512]{1,0:T(4,128)} %copy-done.38) | copy-start | bytes 24580 | tf_op jit(solution)/shard_map/while/body/eval_jaxpr/while
  858.7 130.7 %reduce-scatter.16.cloned.1.call-start = ((), (), s32[]{:S(2)}) async-start(), calls=%async_computation.18 | async-start | bytes 1769472 | tf_op jit(solution)/shard_map/reduce_scatter | solution.py:272
  870.1 165.4 %reduce-scatter.14.cloned.1.call-start = ((), (), s32[]{:S(2)}) async-start(), calls=%async_computation.17 | async-start | bytes 5242880 | tf_op jit(solution)/shard_map/reduce_scatter | solution.py:263
  877.2 158.3 %copy-start.3 = (bf16[512,1024]{1,0:T(8,128)(2,1)S(1)}, bf16[512,1024]{1,0:T(8,128)(2,1)}, u32[]{:S(2)}) copy-start(bf16[512,1024]{1,0:T(8,128)(2,1)} %param.22) | copy-start | bytes 3145732
  877.2 158.3 %copy-start.37 = (f32[1,1024]{1,0:T(1,128)S(1)}, f32[1,1024]{1,0:T(1,128)}, u32[]{:S(2)}) copy-start(f32[1,1024]{1,0:T(1,128)} %copy-done.36) | copy-start | bytes 12292
  877.2 158.3 %copy-start.41 = (f32[512]{0:T(512)S(1)}, f32[512]{0:T(512)}, u32[]{:S(2)}) copy-start(f32[512]{0:T(512)} %copy-done.40) | copy-start | bytes 6148
  877.2 160.1 %copy-start.48 = (f32[512]{0:T(512)S(1)}, f32[512]{0:T(512)}, u32[]{:S(2)}) copy-start(f32[512]{0:T(512)} %copy-done.47) | copy-start | bytes 6148
  877.2 160.1 %copy-start.44 = (f32[512]{0:T(512)S(1)}, f32[512]{0:T(512)}, u32[]{:S(2)}) copy-start(f32[512]{0:T(512)} %copy-done.43) | copy-start | bytes 6148
  877.2 162.5 %copy-start.49 = (f32[1024]{0:T(1024)S(1)}, f32[1024]{0:T(1024)}, u32[]{:S(2)}) copy-start(f32[1024]{0:T(1024)} %get-tuple-element.261) | copy-start | bytes 12292
  877.2 204.3 %copy-start.42 = (f32[2,1024]{1,0:T(2,128)S(1)}, f32[2,1024]{1,0:T(2,128)}, u32[]{:S(2)}) copy-start(f32[2,1024]{1,0:T(2,128)} %param.37) | copy-start | bytes 24580
  877.2 204.3 %copy-start.50 = (f32[2,1024]{1,0:T(2,128)S(1)}, f32[2,1024]{1,0:T(2,128)}, u32[]{:S(2)}) copy-start(f32[2,1024]{1,0:T(2,128)} %param.38) | copy-start | bytes 24580
  877.2 204.3 %copy-start.51 = (f32[2,1024]{1,0:T(2,128)S(1)}, f32[2,1024]{1,0:T(2,128)}, u32[]{:S(2)}) copy-start(f32[2,1024]{1,0:T(2,128)} %param.39) | copy-start | bytes 24580
  877.3 204.9 %copy-start.7 = (f32[512,1024]{1,0:T(8,128)S(1)}, f32[512,1024]{1,0:T(8,128)}, u32[]{:S(2)}) copy-start(f32[512,1024]{1,0:T(8,128)} %copy-done.6) | copy-start | bytes 6291460
  877.3 204.9 %copy-start.46 = (f32[512]{0:T(512)S(1)}, f32[512]{0:T(512)}, u32[]{:S(2)}) copy-start(f32[512]{0:T(512)} %copy-done.45) | copy-start | bytes 6148
  1086.3 7.4 copy-start.20
  1086.3 7.4 copy-start.26
  1086.3 8.6 copy-start.17
  1086.3 8.6 copy-start.25
  1086.4 8.6 copy-start.27
  1086.4 8.6 copy-start.28
  (41 other events, 149.8 us)
Sparse Core Ops, SparseCore 0:
  10.7 50.9 all-gather.9
  63.8 33.7 all-gather.7
  176.1 71.7 reduce-scatter.7
  250.6 73.3 all-gather.13
  326.1 32.7 all-gather.11
  361.7 49.2 all-gather.15
  412.6 32.9 all-gather.17
  478.0 44.5 reduce-scatter.11
  525.1 44.5 reduce-scatter.9
  575.9 34.4 all-gather.19
  614.5 156.3 all-reduce.9
  774.7 66.9 reduce-scatter.19
  858.9 62.1 reduce-scatter.17
  925.0 64.4 reduce-scatter.15
  992.0 43.4 reduce-scatter.13
where the time goes:
time: 1110 us; the launch traced here: 1100 us
  waiting for transfers between devices  510 us (46%)
  matrix products  283 us (25%)
  other arithmetic  125 us (11%)
  local copies, waits for them, and re-layouts  88.5 us (8%)
  blocking collectives  76 us (7%)
  between operations  20.7 us (2%)
    all_gather x1, waiting for transfers between devices, per_device(): lax.all_gather(in_master.astype(jnp.bfloat16), 'dp', axis=0, tiled=True)  69.7 us
    reduce_scatter x1, waiting for transfers between devices, per_device(): lax.psum_scatter(jnp.dot(attended, w_out, preferred_element_type=jnp.floa...  69.5 us
    reduce_scatter x1, waiting for transfers between devices, per_device(): lax.psum_scatter(grad_qkv.reshape(D, 3, width_local).astype(jnp.bfloat16)...  66.9 us
    dynamic_update_slice x8, local copies, waits for them, and re-layouts, backward_row(): lax.scan(backward_block, (zeros_acc, zeros_acc), block_inputs)  46.6 us
    dot_general x4, matrix products, backward_block(): jnp.einsum('qhd,khd->hqk', grad_block, value_row, preferred_element_type=...  46.1 us
    reduce_scatter x1, waiting for transfers between devices, per_device(): lax.psum_scatter(jnp.dot(hidden, w_down, preferred_element_type=jnp.float...  44.4 us
    convert_element_type x4, other arithmetic, backward_block(): score_grad = (probs_block * (prob_grad - row_inner)).astype(jnp.bfloat16)  44.2 us
    dot_general x4, matrix products, contract_cols(): lax.dot_general(left, right, (((1,), (1,)), ((), ())), preferred_element_...  43.7 us
  transfers between devices with their start and end apart: 15, of which 13 were waited for; matrix products, arithmetic and copies ran while one was open for 32% of the time, Pallas kernels for 0%

commit v1 on v0

--- a/solution.py
+++ b/solution.py
@@ -188,7 +188,14 @@
     ).astype(jnp.float32)
     layer_out = output.astype(jnp.bfloat16)
     upstream = cotangent.astype(jnp.float32)
-    gathered_down = lax.all_gather(cotangent, "tensor", axis=0, tiled=True)
+    ring = [cotangent]
+    for hop in range(3):
+        ring.append(lax.ppermute(ring[-1], "tensor", [(dev, (dev + 1) % 4) for dev in range(4)]))
+    gathered_down = jnp.roll(
+        jnp.concatenate(ring[::-1], axis=0),
+        (lax.axis_index("tensor") + 1) * ring[0].shape[0],
+        axis=0,
+    )
     grad_down = contract_rows(hidden, gathered_down)
     hidden_grad = contract_cols(gathered_down, w_down)
     gate_up_grad = jax.vjp(swiglu, gate_up)[1](hidden_grad)[0].astype(jnp.bfloat16)

time: 1110 us -> 1070 us (0.964)
  waiting for transfers between devices: 510 us -> 459 us
  local copies, waits for them, and re-layouts: 88.5 us -> 103 us
    all_gather x1, waiting for transfers between devices: 69.7 us -> 14.6 us  [per_device(): lax.all_gather(in_master.astype(jnp.bfloat16), 'dp', axis=0, tiled=True)]
    ppermute x0 -> x3, waiting for transfers between devices: none -> 41.4 us  [per_device(): lax.ppermute(ring[-1], 'tensor', [(dev, (dev + 1) % 4) for dev in range(4)])]
    all_gather x1 -> x0, waiting for transfers between devices: 34.6 us -> none  [per_device(): gathered_down = lax.all_gather(cotangent, 'tensor', axis=0, tiled=True)]
    unnamed x106 -> x119, local copies, waits for them, and re-layouts: 16.9 us -> 30.3 us
  transfers between devices with their start and end apart: 15 -> 17, of which waited for: 13 -> 14; matrix products, arithmetic and copies ran while one was open for 32% -> 34% of each run, Pallas kernels for 0% -> 0%
where the time goes in v1:
time: 1070 us
  waiting for transfers between devices  459 us (43%)
  matrix products  283 us (26%)
  other arithmetic  125 us (12%)
  local copies, waits for them, and re-layouts  103 us (10%)
  blocking collectives  76 us (7%)
  between operations  20.7 us (2%)
    reduce_scatter x1, waiting for transfers between devices, per_device(): lax.psum_scatter(jnp.dot(attended, w_out, preferred_element_type=jnp.floa...  69.5 us
    reduce_scatter x1, waiting for transfers between devices, per_device(): lax.psum_scatter(grad_qkv.reshape(D, 3, width_local).astype(jnp.bfloat16)...  67.1 us
    dynamic_update_slice x8, local copies, waits for them, and re-layouts, backward_row(): lax.scan(backward_block, (zeros_acc, zeros_acc), block_inputs)  46.6 us
    dot_general x4, matrix products, backward_block(): jnp.einsum('qhd,khd->hqk', grad_block, value_row, preferred_element_type=...  46.1 us
    reduce_scatter x1, waiting for transfers between devices, per_device(): lax.psum_scatter(jnp.dot(hidden, w_down, preferred_element_type=jnp.float...  44.4 us
    convert_element_type x4, other arithmetic, backward_block(): score_grad = (probs_block * (prob_grad - row_inner)).astype(jnp.bfloat16)  44.4 us
    dot_general x4, matrix products, contract_cols(): lax.dot_general(left, right, (((1,), (1,)), ((), ())), preferred_element_...  43.7 us
    reduce_scatter x1, waiting for transfers between devices, per_device(): lax.psum_scatter(contract_cols(qkv_grad_low, w_qkv).astype(jnp.bfloat16),...  41.8 us
  transfers between devices with their start and end apart: 17, of which 14 were waited for; matrix products, arithmetic and copies ran while one was open for 34% of the time, Pallas kernels for 0%

profile of v1, /device:TPU:0, one launch (start us, length us, event | category | flops | bytes accessed | tf_op | source)
XLA Modules:
  0.0 1068.7 jit_solution(3535157948318641558)
XLA Ops:
  16.8 36.3 %all_gather.23 = bf16[256,1024]{1,0:T(8,128)(2,1)} all-gather(bf16[32,1024]{1,0:T(8,128)(2,1)S(1)} %convert_element_type.159), channel_id=1, replica_groups=mesh['dp'=8,'tensor'=4] {'dp'}, dimensions={0}, use_global_device_ids=true | all-gather | bytes 589824 | tf_op jit(solution)/shard_map/all_gather | solution.py:120
  54.1 7.5 all-gather.9.cloned.1.call-done
  61.6 35.9 %all-gather.7.cloned.1.call-done = bf16[2048,1024]{1,0:T(8,128)(2,1)} async-done(((bf16[512,1024]{1,0:T(8,128)(2,1)}), bf16[2048,1024]{1,0:T(8,128)(2,1)}) %all-gather.7.cloned.1.call-update) | async-done | bytes 4194320 | tf_op jit(solution)/shard_map/all_gather | solution.py:132
  97.5 6.2 fusion.48
  110.1 57.2 %while.47 = (s32[]{:T(128)}, bf16[4,512,4,64]{1,3,2,0:T(8,128)(2,1)}, f32[4,4,512,1]{2,1,3,0:T(4,128)}, s32[4,512]{1,0:T(4,128)S(1)}, s32[2048]{0:T(1024)S(1)}, ...) while((s32[]{:T(128)}, ...), condition=%wide.region_8.9_spmd, body=%wide.region_5.8_spmd.sunk | while | flops 1121056768 | bytes 57227380 | solution.py:163
  178.5 69.5 %reduce-scatter.8.cloned.1.call-done = f32[512,1024]{1,0:T(8,128)} async-done(((f32[2048,1024]{1,0:T(8,128)}), f32[512,1024]{1,0:T(8,128)}) %reduce-scatter.8.cloned.1.call-update) | async-done | bytes 2097168 | tf_op jit(solution)/shard_map/reduce_scatter | solution.py:173
  251.9 14.4 %collective-permute-done = bf16[512,1024]{1,0:T(8,128)(2,1)S(1)} collective-permute-done((bf16[512,1024]{1,0:T(8,128)(2,1)}, bf16[512,1024]{1,0:T(8,128)(2,1)S(1)}, u32[]{:S(2)}, u32[]{:S(2)}) %collective-permute-start) | collective-permute-done | bytes 1048608 | tf_op jit(solution)/shard_map/ppermute | solution.py:193
  267.3 14.3 %collective-permute-done.1 = bf16[512,1024]{1,0:T(8,128)(2,1)} collective-permute-done((bf16[512,1024]{1,0:T(8,128)(2,1)S(1)}, bf16[512,1024]{1,0:T(8,128)(2,1)}, u32[]{:S(2)}, u32[]{:S(2)}) %collective-permute-start.1) | collective-permute-done | bytes 1048608 | tf_op jit(solution)/shard_map/ppermute | solution.py:193
  283.5 12.6 %collective-permute-done.2 = bf16[512,1024]{1,0:T(8,128)(2,1)} collective-permute-done((bf16[512,1024]{1,0:T(8,128)(2,1)}, bf16[512,1024]{1,0:T(8,128)(2,1)}, u32[]{:S(2)}, u32[]{:S(2)}) %collective-permute-start.2) | collective-permute-done | bytes 1048608 | tf_op jit(solution)/shard_map/ppermute | solution.py:193
  309.5 14.6 %all-gather.13.cloned.1.call-done = bf16[1024,2,1024]{2,1,0:T(2,128)(2,1)} async-done(((bf16[128,2,1024]{2,1,0:T(2,128)(2,1)}), bf16[1024,2,1024]{2,1,0:T(2,128)(2,1)}) %all-gather.13.cloned.1.call-update) | async-done | bytes 4194320 | tf_op jit(solution)/shard_map/all_gather | solution.py:121
  329.8 29.2 %all-gather.11.cloned.1.call-done = bf16[2048,1024]{1,0:T(8,128)(2,1)} async-done(((bf16[512,1024]{1,0:T(8,128)(2,1)}), bf16[2048,1024]{1,0:T(8,128)(2,1)}) %all-gather.11.cloned.1.call-update) | async-done | bytes 4194320 | tf_op jit(solution)/shard_map/all_gather | solution.py:180
  359.0 15.2 %fusion.105 = f32[2048,2048]{1,0:T(8,128)} fusion(bf16[2048,1024]{1,0:T(8,128)(2,1)} %all-gather.11.cloned.1.call-done, bf16[1024,2048]{1,0:T(8,128)(2,1)} %bitcast.174), kind=kOutput, calls=%fused_computation.194 | convolution fusion | flops 8589934592 | bytes 25165824 | tf_op jit(solution)/shard_map/dot_general | solution.py:181
  374.2 36.9 %all-gather.15.cloned.1.call-done = bf16[1024,1024]{1,0:T(8,128)(2,1)} async-done(((bf16[128,1024]{1,0:T(8,128)(2,1)}), bf16[1024,1024]{1,0:T(8,128)(2,1)}) %all-gather.15.cloned.1.call-update) | async-done | bytes 2097168 | tf_op jit(solution)/shard_map/all_gather | solution.py:122
  411.1 17.2 %fusion.80 = (f32[2048,1024]{1,0:T(8,128)}, f32[2048,1024]{1,0:T(8,128)}, bf16[2048,1024]{1,0:T(8,128)(2,1)}) fusion(f32[2048,2048]{1,0:T(8,128)} %fusion.105, bf16[1024,1024]{1,0:T(8,128)(2,1)} %all-gather.15.cloned.1.call-done, bf16[4096,1024]{1,0:T(8,128)(2,1)} %constant_dynamic-update-slice_fusion, s32[]{:T(128)S(6)} %select_n.21), kind=kOutput, calls=%fused_computation.128 | convolution fusion | flops 4324327424 | bytes 44040196 | tf_op jit(solution)/shard_map/dot_general | solution.py:85
  428.3 15.1 %convolution_convert_fusion.1 = bf16[2048,1024]{1,0:T(8,128)(2,1)} fusion(bf16[1024,2048]{1,0:T(8,128)(2,1)} %bitcast.175, f32[2048,1024]{1,0:T(8,128)} %get-tuple-element.338, f32[2048,1024]{1,0:T(8,128)} %get-tuple-element.337), kind=kOutput, calls=%fused_computation.65 | convolution fusion | flops 8600420352 | bytes 25165824 | tf_op jit(solution)/shard_map/dot_general | solution.py:85
  443.8 9.4 convolution_convert_fusion.3
  453.3 33.2 %reduce-scatter.12.cloned.1.call-done = bf16[512,1024]{1,0:T(8,128)(2,1)} async-done(((bf16[2048,1024]{1,0:T(8,128)(2,1)}), bf16[512,1024]{1,0:T(8,128)(2,1)}) %reduce-scatter.12.cloned.1.call-update) | async-done | bytes 1048592 | tf_op jit(solution)/shard_map/reduce_scatter | solution.py:203
  489.2 44.4 %reduce-scatter.10.cloned.1.call-done = bf16[512,1024]{1,0:T(8,128)(2,1)} async-done(((bf16[2048,1024]{1,0:T(8,128)(2,1)}), bf16[512,1024]{1,0:T(8,128)(2,1)}) %reduce-scatter.10.cloned.1.call-update) | async-done | bytes 1048592 | tf_op jit(solution)/shard_map/reduce_scatter | solution.py:183
  539.8 17.1 %convolution_convert_fusion = bf16[1024,2048]{1,0:T(8,128)(2,1)} fusion(bf16[2048,1024]{1,0:T(8,128)(2,1)} %all-gather.11.cloned.1.call-done, f32[2048,1024]{1,0:T(8,128)} %get-tuple-element.338, f32[2048,1024]{1,0:T(8,128)} %get-tuple-element.337), kind=kOutput, calls=%fused_computation.64 | convolution fusion | flops 8600420352 | bytes 25165824 | tf_op jit(solution)/shard_map/dot_general | solution.py:79
  556.8 7.9 convert_element_type.182
  564.8 9.5 fusion.69
  584.5 230.3 %while.48 = (s32[]{:T(128)}, f32[2048,4,64]{0,2,1:T(8,128)}, f32[2048,4,64]{0,2,1:T(8,128)}, f32[4,512,4,64]{1,0,3,2:T(4,128)}, bf16[4,512,4,64]{1,3,2,0:T(8,128...) while((s32[]{:T(128)}, f32[2048,4,64]{0,2,1:T(8,128)}, ...), condition=%wide.region_18.19_spmd.clone, body=%wide.region_16.18_spmd.clone.sunk | while | flops 2751068160 | bytes 183179600 | solution.py:253
  589.6 7.2 fusion.163
  596.9 11.5 %multiply_reduce_fusion.4 = (f32[4,512]{1,0:T(4,128)}, f32[4,512,2048]{2,1,0:T(8,128)}) fusion(f32[4,512,2048]{2,1,0:T(8,128)S(1)} %fusion.161, f32[4,512]{1,0:T(4,128)S(1)} %dynamic-slice_bitcast_fusion.2, pred[512,2048]{1,0:T(8,128)(4,1)} %copy-done.1, bf16[2048,4,64]{0,2,1:T(8,128)(2,1)} %get-tuple-element.552, ...), kind=kOutput, calls=%fused_computation.20.clone.1 | convolution fusion | flops 557840384 | bytes 35930116 | tf_op jit(solution)/shard_map/while/body/eval_jaxpr/while/body/eval_jaxpr/qhd,khd->hqk/dot_general | solution.py:225
  608.4 11.2 %multiply_convert_fusion.4 = bf16[4,512,2048]{2,1,0:T(8,128)(2,1)} fusion(f32[4,512,2048]{2,1,0:T(8,128)} %get-tuple-element.487, f32[4,512,2048]{2,1,0:T(8,128)S(1)} %fusion.161, f32[4,512]{1,0:T(4,128)} %get-tuple-element.488, f32[4,512]{1,0:T(4,128)S(1)} %dynamic-slice_bitcast_fusion.2, pred[512,2048]{1,0:T(8,128)(4,1)} %copy-done.1), kind=kLoop, calls=%fused_computation.19.clone.1 | loop fusion | flops 25165824 | bytes 43008000 | tf_op jit(solution)/shard_map/while/body/eval_jaxpr/while/body/eval_jaxpr/convert_element_type | solution.py:229
  619.5 6.2 fusion.164
  630.2 11.1 %dynamic_update_slice.33 = f32[4,512,4,64]{1,0,3,2:T(4,128)} dynamic-update-slice(f32[4,512,4,64]{1,0,3,2:T(4,128)} %get-tuple-element.532, f32[1,512,4,64]{1,0,3,2:T(1,128)S(1)} %copy.107, s32[]{:T(128)S(6)} %copy.132, s32[]{:T(128)} %constant.107.clone.1..sunk, s32[]{:T(128)} %constant.107.clone.1..sunk, s32[]{:T(128)} %constant.107.clone.1..sunk) | dynamic-update-slice | bytes 1048580 | tf_op jit(solution)/shard_map/while/body/eval_jaxpr/while/body/jit(dynamic_update_index_in_dim)/dynamic_update_slice | solution.py:253
  646.3 7.6 fusion.163
  654.0 11.5 %multiply_reduce_fusion.4 = (f32[4,512]{1,0:T(4,128)}, f32[4,512,2048]{2,1,0:T(8,128)}) fusion(f32[4,512,2048]{2,1,0:T(8,128)S(1)} %fusion.161, f32[4,512]{1,0:T(4,128)S(1)} %dynamic-slice_bitcast_fusion.2, pred[512,2048]{1,0:T(8,128)(4,1)} %copy-done.1, bf16[2048,4,64]{0,2,1:T(8,128)(2,1)} %get-tuple-element.552, ...), kind=kOutput, calls=%fused_computation.20.clone.1 | convolution fusion | flops 557840384 | bytes 35930116 | tf_op jit(solution)/shard_map/while/body/eval_jaxpr/while/body/eval_jaxpr/qhd,khd->hqk/dot_general | solution.py:225
  665.5 11.1 %multiply_convert_fusion.4 = bf16[4,512,2048]{2,1,0:T(8,128)(2,1)} fusion(f32[4,512,2048]{2,1,0:T(8,128)} %get-tuple-element.487, f32[4,512,2048]{2,1,0:T(8,128)S(1)} %fusion.161, f32[4,512]{1,0:T(4,128)} %get-tuple-element.488, f32[4,512]{1,0:T(4,128)S(1)} %dynamic-slice_bitcast_fusion.2, pred[512,2048]{1,0:T(8,128)(4,1)} %copy-done.1), kind=kLoop, calls=%fused_computation.19.clone.1 | loop fusion | flops 25165824 | bytes 43008000 | tf_op jit(solution)/shard_map/while/body/eval_jaxpr/while/body/eval_jaxpr/convert_element_type | solution.py:229
  676.6 6.2 fusion.164
  688.1 11.1 %dynamic_update_slice.33 = f32[4,512,4,64]{1,0,3,2:T(4,128)} dynamic-update-slice(f32[4,512,4,64]{1,0,3,2:T(4,128)} %get-tuple-element.532, f32[1,512,4,64]{1,0,3,2:T(1,128)S(1)} %copy.107, s32[]{:T(128)S(6)} %copy.132, s32[]{:T(128)} %constant.107.clone.1..sunk, s32[]{:T(128)} %constant.107.clone.1..sunk, s32[]{:T(128)} %constant.107.clone.1..sunk) | dynamic-update-slice | bytes 1048580 | tf_op jit(solution)/shard_map/while/body/eval_jaxpr/while/body/jit(dynamic_update_index_in_dim)/dynamic_update_slice | solution.py:253
  704.2 7.6 fusion.163
  711.8 11.5 %multiply_reduce_fusion.4 = (f32[4,512]{1,0:T(4,128)}, f32[4,512,2048]{2,1,0:T(8,128)}) fusion(f32[4,512,2048]{2,1,0:T(8,128)S(1)} %fusion.161, f32[4,512]{1,0:T(4,128)S(1)} %dynamic-slice_bitcast_fusion.2, pred[512,2048]{1,0:T(8,128)(4,1)} %copy-done.1, bf16[2048,4,64]{0,2,1:T(8,128)(2,1)} %get-tuple-element.552, ...), kind=kOutput, calls=%fused_computation.20.clone.1 | convolution fusion | flops 557840384 | bytes 35930116 | tf_op jit(solution)/shard_map/while/body/eval_jaxpr/while/body/eval_jaxpr/qhd,khd->hqk/dot_general | solution.py:225
  723.3 11.1 %multiply_convert_fusion.4 = bf16[4,512,2048]{2,1,0:T(8,128)(2,1)} fusion(f32[4,512,2048]{2,1,0:T(8,128)} %get-tuple-element.487, f32[4,512,2048]{2,1,0:T(8,128)S(1)} %fusion.161, f32[4,512]{1,0:T(4,128)} %get-tuple-element.488, f32[4,512]{1,0:T(4,128)S(1)} %dynamic-slice_bitcast_fusion.2, pred[512,2048]{1,0:T(8,128)(4,1)} %copy-done.1), kind=kLoop, calls=%fused_computation.19.clone.1 | loop fusion | flops 25165824 | bytes 43008000 | tf_op jit(solution)/shard_map/while/body/eval_jaxpr/while/body/eval_jaxpr/convert_element_type | solution.py:229
  734.4 6.2 fusion.164
  745.8 11.1 %dynamic_update_slice.33 = f32[4,512,4,64]{1,0,3,2:T(4,128)} dynamic-update-slice(f32[4,512,4,64]{1,0,3,2:T(4,128)} %get-tuple-element.532, f32[1,512,4,64]{1,0,3,2:T(1,128)S(1)} %copy.107, s32[]{:T(128)S(6)} %copy.132, s32[]{:T(128)} %constant.107.clone.1..sunk, s32[]{:T(128)} %constant.107.clone.1..sunk, s32[]{:T(128)} %constant.107.clone.1..sunk) | dynamic-update-slice | bytes 1048580 | tf_op jit(solution)/shard_map/while/body/eval_jaxpr/while/body/jit(dynamic_update_index_in_dim)/dynamic_update_slice | solution.py:253
  761.9 7.6 fusion.163
  769.5 11.5 %multiply_reduce_fusion.4 = (f32[4,512]{1,0:T(4,128)}, f32[4,512,2048]{2,1,0:T(8,128)}) fusion(f32[4,512,2048]{2,1,0:T(8,128)S(1)} %fusion.161, f32[4,512]{1,0:T(4,128)S(1)} %dynamic-slice_bitcast_fusion.2, pred[512,2048]{1,0:T(8,128)(4,1)} %copy-done.1, bf16[2048,4,64]{0,2,1:T(8,128)(2,1)} %get-tuple-element.552, ...), kind=kOutput, calls=%fused_computation.20.clone.1 | convolution fusion | flops 557840384 | bytes 35930116 | tf_op jit(solution)/shard_map/while/body/eval_jaxpr/while/body/eval_jaxpr/qhd,khd->hqk/dot_general | solution.py:225
  781.0 11.1 %multiply_convert_fusion.4 = bf16[4,512,2048]{2,1,0:T(8,128)(2,1)} fusion(f32[4,512,2048]{2,1,0:T(8,128)} %get-tuple-element.487, f32[4,512,2048]{2,1,0:T(8,128)S(1)} %fusion.161, f32[4,512]{1,0:T(4,128)} %get-tuple-element.488, f32[4,512]{1,0:T(4,128)S(1)} %dynamic-slice_bitcast_fusion.2, pred[512,2048]{1,0:T(8,128)(4,1)} %copy-done.1), kind=kLoop, calls=%fused_computation.19.clone.1 | loop fusion | flops 25165824 | bytes 43008000 | tf_op jit(solution)/shard_map/while/body/eval_jaxpr/while/body/eval_jaxpr/convert_element_type | solution.py:229
  792.1 6.2 fusion.164
  803.5 11.1 %dynamic_update_slice.33 = f32[4,512,4,64]{1,0,3,2:T(4,128)} dynamic-update-slice(f32[4,512,4,64]{1,0,3,2:T(4,128)} %get-tuple-element.532, f32[1,512,4,64]{1,0,3,2:T(1,128)S(1)} %copy.107, s32[]{:T(128)S(6)} %copy.132, s32[]{:T(128)} %constant.107.clone.1..sunk, s32[]{:T(128)} %constant.107.clone.1..sunk, s32[]{:T(128)} %constant.107.clone.1..sunk) | dynamic-update-slice | bytes 1048580 | tf_op jit(solution)/shard_map/while/body/eval_jaxpr/while/body/jit(dynamic_update_index_in_dim)/dynamic_update_slice | solution.py:253
  834.4 7.0 convolution_convert_fusion.2
  847.8 37.4 %reduce-scatter.18.cloned.1.call-done = bf16[32,1024]{1,0:T(8,128)(2,1)} async-done(((bf16[256,1024]{1,0:T(8,128)(2,1)}), bf16[32,1024]{1,0:T(8,128)(2,1)}) %reduce-scatter.18.cloned.1.call-update) | async-done | bytes 65552 | tf_op jit(solution)/shard_map/reduce_scatter | solution.py:285
  886.6 67.1 %reduce-scatter.16.cloned.1.call-done = bf16[128,3,256]{2,0,1:T(8,128)(2,1)} async-done(((bf16[1024,3,256]{2,0,1:T(8,128)(2,1)}), bf16[128,3,256]{2,0,1:T(8,128)(2,1)}) %reduce-scatter.16.cloned.1.call-update) | async-done | bytes 196624 | tf_op jit(solution)/shard_map/reduce_scatter | solution.py:279
  958.0 41.8 %reduce-scatter.14.cloned.1.call-done = bf16[512,1024]{1,0:T(8,128)(2,1)} async-done(((bf16[2048,1024]{1,0:T(8,128)(2,1)}), bf16[512,1024]{1,0:T(8,128)(2,1)}) %reduce-scatter.14.cloned.1.call-update) | async-done | bytes 1048592 | tf_op jit(solution)/shard_map/reduce_scatter | solution.py:270
  1004.0 39.8 %all-reduce.7 = (f32[]{:T(128)}, f32[2,1024]{1,0:T(2,128)S(1)}) all-reduce(f32[]{:T(128)S(6)} %add.226, f32[2,1024]{1,0:T(2,128)S(1)} %pad_maximum_fusion.1), channel_id=1, replica_groups=mesh['dp'=8,'tensor'=4] {'dp','tensor'}, use_global_device_ids=true, to_apply=%region_30.31 | all-reduce | flops 2049 | bytes 16392 | tf_op jit(solution)/shard_map/psum | solution.py:305
  1050.6 6.5 multiply_subtract_fusion
  (314 shorter events, 211.4 us)
Async XLA Ops:
  7.2 9.1 copy-start.55
  7.2 9.6 copy-start.32
  7.2 54.4 %all-gather.9.cloned.1.call-start = ((), (), s32[]{:S(2)}) async-start(), calls=%async_computation.8 | async-start | bytes 1769472 | tf_op jit(solution)/shard_map/all_gather | solution.py:119
  9.1 88.4 %all-gather.7.cloned.1.call-start = ((), (), s32[]{:S(2)}) async-start(), calls=%async_computation.7 | async-start | bytes 5242880 | tf_op jit(solution)/shard_map/all_gather | solution.py:132
  16.3 231.7 %reduce-scatter.8.cloned.1.call-start = ((), (), s32[]{:S(2)}) async-start(), calls=%async_computation.9 | async-start | bytes 10485760 | tf_op jit(solution)/shard_map/reduce_scatter | solution.py:173
  54.1 50.3 %copy-start.17 = (f32[2048,32]{0,1:T(8,128)}, f32[2048,32]{0,1:T(8,128)S(1)}, u32[]{:S(2)}) copy-start(f32[2048,32]{0,1:T(8,128)S(1)} %get-tuple-element.355) | copy-start | bytes 786436
  54.1 50.3 %copy-start.19 = (f32[2048,32]{0,1:T(8,128)}, f32[2048,32]{0,1:T(8,128)S(1)}, u32[]{:S(2)}) copy-start(f32[2048,32]{0,1:T(8,128)S(1)} %get-tuple-element.356) | copy-start | bytes 786436
  167.3 8.7 copy-start.4
  167.3 8.7 copy-start.5
  176.1 148.1 %all-gather.13.cloned.1.call-start = ((), (), s32[]{:S(2)}) async-start(), calls=%async_computation.11 | async-start | bytes 4718592 | tf_op jit(solution)/shard_map/all_gather | solution.py:121
  178.4 180.5 %all-gather.11.cloned.1.call-start = ((), (), s32[]{:S(2)}) async-start(), calls=%async_computation.10 | async-start | bytes 5242880 | tf_op jit(solution)/shard_map/all_gather | solution.py:180
  251.8 159.3 %all-gather.15.cloned.1.call-start = ((), (), s32[]{:S(2)}) async-start(), calls=%async_computation.12 | async-start | bytes 2359296 | tf_op jit(solution)/shard_map/all_gather | solution.py:122
  251.8 14.5 %collective-permute-start = (bf16[512,1024]{1,0:T(8,128)(2,1)}, bf16[512,1024]{1,0:T(8,128)(2,1)S(1)}, u32[]{:S(2)}, u32[]{:S(2)}) collective-permute-start(bf16[512,1024]{1,0:T(8,128)(2,1)} %param.23), channel_id=1, source_target_pairs={{0,1},{1,2},{2,3},{3,0},{4,5},{5,6},{6,7},{7,4},{8,9},{9,10},{10,1... | collective-permute-start | bytes 3145736 | tf_op jit(solution)/shard_map/ppermute | solution.py:193
  267.3 14.3 %collective-permute-start.1 = (bf16[512,1024]{1,0:T(8,128)(2,1)S(1)}, bf16[512,1024]{1,0:T(8,128)(2,1)}, u32[]{:S(2)}, u32[]{:S(2)}) collective-permute-start(bf16[512,1024]{1,0:T(8,128)(2,1)S(1)} %collective-permute-done), channel_id=1, source_target_pairs={{0,1},{1,2},{2,3},{3,0},{4,5},{5,6},{6,7},{7,4},{8,9},{9,10},{10,1... | collective-permute-start | bytes 3145736 | tf_op jit(solution)/shard_map/ppermute | solution.py:193
  281.6 14.5 %collective-permute-start.2 = (bf16[512,1024]{1,0:T(8,128)(2,1)}, bf16[512,1024]{1,0:T(8,128)(2,1)}, u32[]{:S(2)}, u32[]{:S(2)}) collective-permute-start(bf16[512,1024]{1,0:T(8,128)(2,1)} %collective-permute-done.1), channel_id=1, source_target_pairs={{0,1},{1,2},{2,3},{3,0},{4,5},{5,6},{6,7},{7,4},{8,9},{9,10},{10,1... | collective-permute-start | bytes 3145736 | tf_op jit(solution)/shard_map/ppermute | solution.py:193
  283.4 203.1 %reduce-scatter.12.cloned.1.call-start = ((), (), s32[]{:S(2)}) async-start(), calls=%async_computation.14 | async-start | bytes 5242880 | tf_op jit(solution)/shard_map/reduce_scatter | solution.py:203
  283.5 17.2 %copy-start.15 = (bf16[512,1024]{1,0:T(8,128)(2,1)S(1)}, bf16[512,1024]{1,0:T(8,128)(2,1)}, u32[]{:S(2)}) copy-start(bf16[512,1024]{1,0:T(8,128)(2,1)} %copy-done.14) | copy-start | bytes 3145732
  283.5 18.2 %copy-start.8 = (bf16[512,1024]{1,0:T(8,128)(2,1)S(1)}, bf16[512,1024]{1,0:T(8,128)(2,1)}, u32[]{:S(2)}) copy-start(bf16[512,1024]{1,0:T(8,128)(2,1)} %param.23) | copy-start | bytes 3145732
  443.4 90.3 %reduce-scatter.10.cloned.1.call-start = ((), (), s32[]{:S(2)}) async-start(), calls=%async_computation.13 | async-start | bytes 5242880 | tf_op jit(solution)/shard_map/reduce_scatter | solution.py:183
  453.3 121.1 %all-gather.17.cloned.1.call-start = ((), (), s32[]{:S(2)}) async-start(), calls=%async_computation.15 | async-start | bytes 5242880 | tf_op jit(solution)/shard_map/all_gather | solution.py:211
  537.1 19.8 %copy-start.48 = (f32[512]{0:T(512)}, f32[512]{0:T(512)S(1)}, u32[]{:S(2)}) copy-start(f32[512]{0:T(512)S(1)} %negate_multiply_fusion.1) | copy-start | bytes 6148
  539.7 303.6 %all-reduce.10.cloned.1.call-start = ((), (), s32[]{:S(2)}) async-start(), calls=%async_computation.20 | async-start | bytes 8388608
  564.7 281.4 %reduce-scatter.20.cloned.1.call-start = ((), (), s32[]{:S(2)}) async-start(), calls=%async_computation.19 | async-start | bytes 2359296 | tf_op jit(solution)/shard_map/reduce_scatter | solution.py:294
  564.8 9.6 copy-start.22
  574.3 310.8 %reduce-scatter.18.cloned.1.call-start = ((), (), s32[]{:S(2)}) async-start(), calls=%async_computation.18 | async-start | bytes 589824 | tf_op jit(solution)/shard_map/reduce_scatter | solution.py:285
  625.8 15.6 %copy-start.25 = (s32[2048]{0:T(1024)S(1)}, s32[2048]{0:T(1024)}, u32[]{:S(2)}) copy-start(s32[2048]{0:T(1024)} %copy-done.24) | copy-start | bytes 24580 | tf_op jit(solution)/shard_map/while/body/eval_jaxpr/while
  625.8 15.6 %copy-start.42 = (s32[4,512]{1,0:T(4,128)S(1)}, s32[4,512]{1,0:T(4,128)}, u32[]{:S(2)}) copy-start(s32[4,512]{1,0:T(4,128)} %copy-done.41) | copy-start | bytes 24580 | tf_op jit(solution)/shard_map/while/body/eval_jaxpr/while
  682.8 16.4 %copy-start.25 = (s32[2048]{0:T(1024)S(1)}, s32[2048]{0:T(1024)}, u32[]{:S(2)}) copy-start(s32[2048]{0:T(1024)} %copy-done.24) | copy-start | bytes 24580 | tf_op jit(solution)/shard_map/while/body/eval_jaxpr/while
  682.8 16.4 %copy-start.42 = (s32[4,512]{1,0:T(4,128)S(1)}, s32[4,512]{1,0:T(4,128)}, u32[]{:S(2)}) copy-start(s32[4,512]{1,0:T(4,128)} %copy-done.41) | copy-start | bytes 24580 | tf_op jit(solution)/shard_map/while/body/eval_jaxpr/while
  740.6 16.3 %copy-start.25 = (s32[2048]{0:T(1024)S(1)}, s32[2048]{0:T(1024)}, u32[]{:S(2)}) copy-start(s32[2048]{0:T(1024)} %copy-done.24) | copy-start | bytes 24580 | tf_op jit(solution)/shard_map/while/body/eval_jaxpr/while
  740.6 16.3 %copy-start.42 = (s32[4,512]{1,0:T(4,128)S(1)}, s32[4,512]{1,0:T(4,128)}, u32[]{:S(2)}) copy-start(s32[4,512]{1,0:T(4,128)} %copy-done.41) | copy-start | bytes 24580 | tf_op jit(solution)/shard_map/while/body/eval_jaxpr/while
  798.3 16.3 %copy-start.25 = (s32[2048]{0:T(1024)S(1)}, s32[2048]{0:T(1024)}, u32[]{:S(2)}) copy-start(s32[2048]{0:T(1024)} %copy-done.24) | copy-start | bytes 24580 | tf_op jit(solution)/shard_map/while/body/eval_jaxpr/while
  798.3 16.3 %copy-start.42 = (s32[4,512]{1,0:T(4,128)S(1)}, s32[4,512]{1,0:T(4,128)}, u32[]{:S(2)}) copy-start(s32[4,512]{1,0:T(4,128)} %copy-done.41) | copy-start | bytes 24580 | tf_op jit(solution)/shard_map/while/body/eval_jaxpr/while
  823.0 130.7 %reduce-scatter.16.cloned.1.call-start = ((), (), s32[]{:S(2)}) async-start(), calls=%async_computation.17 | async-start | bytes 1769472 | tf_op jit(solution)/shard_map/reduce_scatter | solution.py:279
  834.4 165.4 %reduce-scatter.14.cloned.1.call-start = ((), (), s32[]{:S(2)}) async-start(), calls=%async_computation.16 | async-start | bytes 5242880 | tf_op jit(solution)/shard_map/reduce_scatter | solution.py:270
  841.4 158.3 %copy-start.3 = (bf16[512,1024]{1,0:T(8,128)(2,1)S(1)}, bf16[512,1024]{1,0:T(8,128)(2,1)}, u32[]{:S(2)}) copy-start(bf16[512,1024]{1,0:T(8,128)(2,1)} %param.22) | copy-start | bytes 3145732
  841.4 158.3 %copy-start.40 = (f32[1,1024]{1,0:T(1,128)S(1)}, f32[1,1024]{1,0:T(1,128)}, u32[]{:S(2)}) copy-start(f32[1,1024]{1,0:T(1,128)} %copy-done.39) | copy-start | bytes 12292
  841.4 158.3 %copy-start.44 = (f32[512]{0:T(512)S(1)}, f32[512]{0:T(512)}, u32[]{:S(2)}) copy-start(f32[512]{0:T(512)} %copy-done.43) | copy-start | bytes 6148
  841.4 160.1 %copy-start.51 = (f32[512]{0:T(512)S(1)}, f32[512]{0:T(512)}, u32[]{:S(2)}) copy-start(f32[512]{0:T(512)} %copy-done.50) | copy-start | bytes 6148
  841.5 160.1 %copy-start.47 = (f32[512]{0:T(512)S(1)}, f32[512]{0:T(512)}, u32[]{:S(2)}) copy-start(f32[512]{0:T(512)} %copy-done.46) | copy-start | bytes 6148
  841.5 162.5 %copy-start.52 = (f32[1024]{0:T(1024)S(1)}, f32[1024]{0:T(1024)}, u32[]{:S(2)}) copy-start(f32[1024]{0:T(1024)} %get-tuple-element.261) | copy-start | bytes 12292
  841.5 204.3 %copy-start.45 = (f32[2,1024]{1,0:T(2,128)S(1)}, f32[2,1024]{1,0:T(2,128)}, u32[]{:S(2)}) copy-start(f32[2,1024]{1,0:T(2,128)} %param.37) | copy-start | bytes 24580
  841.5 204.3 %copy-start.53 = (f32[2,1024]{1,0:T(2,128)S(1)}, f32[2,1024]{1,0:T(2,128)}, u32[]{:S(2)}) copy-start(f32[2,1024]{1,0:T(2,128)} %param.38) | copy-start | bytes 24580
  841.5 204.3 %copy-start.54 = (f32[2,1024]{1,0:T(2,128)S(1)}, f32[2,1024]{1,0:T(2,128)}, u32[]{:S(2)}) copy-start(f32[2,1024]{1,0:T(2,128)} %param.39) | copy-start | bytes 24580
  841.5 204.9 %copy-start.7 = (f32[512,1024]{1,0:T(8,128)S(1)}, f32[512,1024]{1,0:T(8,128)}, u32[]{:S(2)}) copy-start(f32[512,1024]{1,0:T(8,128)} %copy-done.6) | copy-start | bytes 6291460
  841.5 204.9 %copy-start.49 = (f32[512]{0:T(512)S(1)}, f32[512]{0:T(512)}, u32[]{:S(2)}) copy-start(f32[512]{0:T(512)} %copy-done.48) | copy-start | bytes 6148
  1050.6 8.6 copy-start.20
  1050.6 8.6 copy-start.28
  (46 other events, 183.2 us)
Sparse Core Ops, SparseCore 0:
  10.7 50.9 all-gather.8
  63.8 33.7 all-gather.6
  176.2 71.7 reduce-scatter.7
  250.7 73.3 all-gather.12
  326.2 32.7 all-gather.10
  361.7 49.2 all-gather.14
  443.5 42.9 reduce-scatter.11
  489.0 44.5 reduce-scatter.9
  539.9 34.4 all-gather.16
  578.3 156.2 all-reduce.9
  738.6 66.6 reduce-scatter.19
  823.2 61.9 reduce-scatter.17
  889.2 64.5 reduce-scatter.15
  956.3 43.4 reduce-scatter.13
